TPU v7x, 32 devices: a whole 2x2x4 slice. The times are simulated.
32 devices in a mesh: face: 2 (over y), tx: 4 (over z), ty: 4 (over x, core).
Axes of the slice: x: 2, y: 2, z: 4, core: 2. Of those that a mesh axis runs over, the one named last changes fastest.
Arguments:
- probes: float32 [2, 4, 2, 6, 32, 32], P(None, None, 'face', None, 'tx', 'ty'), may hold values from -6 to 6
- background_wind: float32 [2, 2, 6, 32, 32], P(None, 'face', None, 'tx', 'ty'), may hold values from -6 to 6
- layer_mass: float32 [2, 6, 32, 32], P('face', None, 'tx', 'ty'), may hold values from 0.5 to 2
- trajectory_heat_factor: float32 [2, 6, 32, 32], P('face', None, 'tx', 'ty'), may hold values from 0.3 to 3
- spread: float32 [4, 2, 6, 32, 32], P(None, 'face', None, 'tx', 'ty'), may hold values from 0.5 to 2
- inverse_misfit_variance: float32 [4, 2, 6, 32, 32], P(None, 'face', None, 'tx', 'ty'), may hold values from 0.25 to 4
- face_links: int32 [6, 4, 7], replicated, may hold values from -1 to 5, as said below
Outputs:
- applied: float32 [2, 4, 2, 6, 32, 32], P(None, None, 'face', None, 'tx', 'ty')
Inputs may be any that keep to these rules, and one draw needn't show every extreme that they name: `face_links`: the table describes the six panels of a cube, each with a right-handed frame: for panel f and edge e, the panel across it, the edge of that panel which touches f, whether the index along the shared edge runs the other way, and the matrix of entries -1, 0, 1 that carries vector components from that panel's frame into the frame of f.
All inputs are finite; a program needn't handle non-finite values.
Results may differ from a plain program's by a relative error of at most 0.00002.
Values sent between devices are 32-bit elements; how exact they have to be, the bound alone decides.
A program may use at most 64 MiB of HBM per device.

v0:
```python
import jax
import jax.numpy as jnp
from jax import lax
from jax.sharding import PartitionSpec as P

time_increment = 0.3
forward_layout = (("vector", 0), ("vector", 2), ("scalar", 4), ("scalar", 5))
adjoint_layout = (("tensor", 0), ("vector", 4), ("scalar", 6), ("vector", 7))


def padded_2(array, sides, width):
    for axis, dim in sides:
        devices, length = (lax.axis_size(axis), array.shape[dim])
        up = [(i, (i + 1) % devices) for i in range(devices - 1)]
        down = [(j, i) for i, j in up]
        last = lax.slice_in_dim(array, length - width, length, axis=dim)
        leading = lax.slice_in_dim(array, 0, width, axis=dim)
        before = lax.ppermute(last, axis, up)
        after = lax.ppermute(leading, axis, down)
        array = jnp.concatenate([before, array, after], axis=dim)
    return array


def carried_in(value, axis, join, neutral, backward):
    count, mine = (lax.axis_size(axis), lax.axis_index(axis))
    pieces = lax.all_gather(value, axis)
    if backward:
        pieces = pieces[::-1]
        mine = count - 1 - mine
    total = jnp.full_like(value, 0) + jnp.asarray(neutral, value.dtype)

    def hop(position, total):
        longer = join(total, pieces[position])
        return jnp.where(position < mine, longer, total)

    return lax.fori_loop(0, count - 1, hop, total)


def carry_pair(leading, trailing, entries):
    return (
        entries[0] * leading + entries[1] * trailing,
        entries[2] * leading + entries[3] * trailing,
    )


def rotate_edge(edge_strip, matrix_codes, layout):
    matrix = matrix_codes.astype(edge_strip.dtype)
    entries = [matrix[:, column].reshape(1, 1, 6, 1) for column in range(4)]
    channels = [edge_strip[number] for number in range(edge_strip.shape[0])]
    for species, offset in layout:
        if species == "vector":
            channels[offset], channels[offset + 1] = carry_pair(
                channels[offset], channels[offset + 1], entries
            )
        elif species == "tensor":
            channels[offset], channels[offset + 1] = carry_pair(
                channels[offset], channels[offset + 1], entries
            )
            channels[offset + 2], channels[offset + 3] = carry_pair(
                channels[offset + 2], channels[offset + 3], entries
            )
            channels[offset], channels[offset + 2] = carry_pair(
                channels[offset], channels[offset + 2], entries
            )
            channels[offset + 1], channels[offset + 3] = carry_pair(
                channels[offset + 1], channels[offset + 3], entries
            )
    return jnp.stack(channels)


def orient(edge_rows, face_links, side, layout):
    source_face = face_links[:, side, 0]
    source_edge = face_links[:, side, 1]
    chosen = edge_rows[:, :, :, source_face, source_edge, :]
    flipped = (face_links[:, side, 2] == 1).reshape(1, 1, 1, 6, 1)
    chosen = jnp.where(flipped, chosen[..., ::-1], chosen)
    return rotate_edge(chosen, face_links[:, side, 3:7], layout)


def face_rows(fields):
    tile_row = lax.axis_index("tx")
    tile_column = lax.axis_index("ty")
    low_rows = jnp.where(tile_row == 0, fields[..., 0, :], 0.0)
    high_rows = jnp.where(tile_row == lax.axis_size("tx") - 1, fields[..., -1, :], 0.0)
    low_columns = jnp.where(tile_column == 0, fields[..., :, 0], 0.0)
    high_columns = jnp.where(tile_column == lax.axis_size("ty") - 1, fields[..., :, -1], 0.0)
    row_pair = jnp.stack([low_rows, high_rows], axis=4)
    column_pair = jnp.stack([low_columns, high_columns], axis=4)
    row_full = lax.psum(lax.all_gather(row_pair, "ty", axis=5, tiled=True), "tx")
    column_full = lax.psum(lax.all_gather(column_pair, "tx", axis=5, tiled=True), "ty")
    return jnp.concatenate([row_full, column_full], axis=4)


def extended_slopes(fields, face_links, layout):
    row_cells = fields.shape[4]
    column_cells = fields.shape[5]
    tile_row = lax.axis_index("tx")
    tile_column = lax.axis_index("ty")
    padded = padded_2(fields, (("tx", 4), ("ty", 5)), 1)
    edge_rows = face_rows(fields)
    western = lax.dynamic_slice_in_dim(
        orient(edge_rows, face_links, 0, layout), tile_column * column_cells, column_cells, 4
    )
    eastern = lax.dynamic_slice_in_dim(
        orient(edge_rows, face_links, 1, layout), tile_column * column_cells, column_cells, 4
    )
    southern = lax.dynamic_slice_in_dim(
        orient(edge_rows, face_links, 2, layout), tile_row * row_cells, row_cells, 4
    )
    northern = lax.dynamic_slice_in_dim(
        orient(edge_rows, face_links, 3, layout), tile_row * row_cells, row_cells, 4
    )
    row_number = lax.broadcasted_iota(jnp.int32, (row_cells, column_cells), 0)
    column_number = lax.broadcasted_iota(jnp.int32, (row_cells, column_cells), 1)
    first_row = (row_number == 0) & (tile_row == 0)
    last_row = (row_number == row_cells - 1) & (tile_row == lax.axis_size("tx") - 1)
    first_column = (column_number == 0) & (tile_column == 0)
    last_column = (column_number == column_cells - 1) & (tile_column == lax.axis_size("ty") - 1)
    east_slope_derivative = 0.5 * (padded[..., 2:, 1:-1] - padded[..., :-2, 1:-1])
    east_slope_derivative = (
        east_slope_derivative
        + jnp.where(last_row, 0.5 * eastern[..., None, :], 0.0)
        - jnp.where(first_row, 0.5 * western[..., None, :], 0.0)
    )
    north_slope_derivative = 0.5 * (padded[..., 1:-1, 2:] - padded[..., 1:-1, :-2])
    north_slope_derivative = (
        north_slope_derivative
        + jnp.where(last_column, 0.5 * northern[..., :, None], 0.0)
        - jnp.where(first_column, 0.5 * southern[..., :, None], 0.0)
    )
    return (east_slope_derivative, north_slope_derivative)


def pressure_of(sheet_depth_state):
    within = jnp.cumsum(sheet_depth_state, axis=1)
    totals_here = within[:, -1]
    underneath = carried_in(totals_here, "face", jnp.add, jnp.zeros_like(totals_here), False)
    return within + underneath[:, None]


def load_of(sensitivity):
    within = jnp.flip(jnp.cumsum(jnp.flip(sensitivity, 1), axis=1), 1)
    totals_here = within[:, 0]
    overhead = carried_in(totals_here, "face", jnp.add, jnp.zeros_like(totals_here), True)
    return within + overhead[:, None]


def body(
    probes,
    background_wind,
    layer_mass,
    trajectory_heat_factor,
    spread,
    inverse_misfit_variance,
    face_links,
):
    normalised_state_array = spread[None] * probes
    west_east_wind_part, south_north_wind_speed, sheet_depth_state, sheet_warmth_state = (
        normalised_state_array[:, 0],
        normalised_state_array[:, 1],
        normalised_state_array[:, 2],
        normalised_state_array[:, 3],
    )
    east_wind_speed, north_wind_speed = (background_wind[0], background_wind[1])
    ground_barometric_load = pressure_of(sheet_depth_state)
    gravity_potential_level = sheet_warmth_state + trajectory_heat_factor * ground_barometric_load
    east_mass_transport = east_wind_speed * sheet_depth_state + layer_mass * west_east_wind_part
    north_mass_transport = (
        north_wind_speed * sheet_depth_state + layer_mass * south_north_wind_speed
    )
    joined_state_arrays = jnp.stack(
        [
            west_east_wind_part,
            south_north_wind_speed,
            east_mass_transport,
            north_mass_transport,
            sheet_warmth_state,
            gravity_potential_level,
        ]
    )
    east_slope_derivative, north_slope_derivative = extended_slopes(
        joined_state_arrays, face_links, forward_layout
    )
    west_east_wind_after = west_east_wind_part - time_increment * (
        east_slope_derivative[5]
        + east_wind_speed * east_slope_derivative[0]
        + north_wind_speed * north_slope_derivative[0]
    )
    south_north_wind_after = south_north_wind_speed - time_increment * (
        north_slope_derivative[5]
        + east_wind_speed * east_slope_derivative[1]
        + north_wind_speed * north_slope_derivative[1]
    )
    depth_after_update = sheet_depth_state - time_increment * (
        east_slope_derivative[2] + north_slope_derivative[3]
    )
    warmth_after_update = sheet_warmth_state - time_increment * (
        east_wind_speed * east_slope_derivative[4] + north_wind_speed * north_slope_derivative[4]
    )
    zonal_cost = inverse_misfit_variance[0] * west_east_wind_after
    meridional_cost = inverse_misfit_variance[1] * south_north_wind_after
    thickness_cost = inverse_misfit_variance[2] * depth_after_update
    heat_misfit_penalty = inverse_misfit_variance[3] * warmth_after_update
    sensitive = jnp.stack(
        [
            east_wind_speed * zonal_cost,
            east_wind_speed * meridional_cost,
            north_wind_speed * zonal_cost,
            north_wind_speed * meridional_cost,
            zonal_cost,
            meridional_cost,
            thickness_cost,
            east_wind_speed * heat_misfit_penalty,
            north_wind_speed * heat_misfit_penalty,
        ]
    )
    east_slope_derivative, north_slope_derivative = extended_slopes(
        sensitive, face_links, adjoint_layout
    )
    geo_back = time_increment * (east_slope_derivative[4] + north_slope_derivative[5])
    flux_east_back = time_increment * east_slope_derivative[6]
    flux_north_back = time_increment * north_slope_derivative[6]
    zonal_back = (
        zonal_cost
        + time_increment * (east_slope_derivative[0] + north_slope_derivative[2])
        + layer_mass * flux_east_back
    )
    meridional_back = (
        meridional_cost
        + time_increment * (east_slope_derivative[1] + north_slope_derivative[3])
        + layer_mass * flux_north_back
    )
    warmth_back = (
        heat_misfit_penalty
        + time_increment * (east_slope_derivative[7] + north_slope_derivative[8])
        + geo_back
    )
    thickness_back = (
        thickness_cost
        + east_wind_speed * flux_east_back
        + north_wind_speed * flux_north_back
        + load_of(trajectory_heat_factor * geo_back)
    )
    adjoint_out = jnp.stack([zonal_back, meridional_back, thickness_back, warmth_back], axis=1)
    return probes + spread[None] * adjoint_out


def solution(mesh):
    return jax.shard_map(
        body,
        mesh=mesh,
        in_specs=(
            P(None, None, "face", None, "tx", "ty"),
            P(None, "face", None, "tx", "ty"),
            P("face", None, "tx", "ty"),
            P("face", None, "tx", "ty"),
            P(None, "face", None, "tx", "ty"),
            P(None, "face", None, "tx", "ty"),
            P(),
        ),
        out_specs=P(None, None, "face", None, "tx", "ty"),
        check_vma=False,
    )
```

profile of v0, /device:TPU:0, one launch (start us, length us, event | category | flops | bytes accessed | tf_op | source)
XLA Modules:
  0.0 178.0 jit_solution(14234062256038518076)
XLA Ops:
  0.0 1.0 copy_multiply_fusion
  1.1 0.8 copy-done.16
  1.8 0.7 copy-done.11
  2.6 5.7 %all-gather = f32[4,1,1,6,8,8]{5,4,3,2,1,0:T(8,128)S(1)} all-gather(f32[2,1,1,6,8,8]{5,4,3,2,1,0:T(8,128)S(1)} %slice_bitcast_fusion.2), channel_id=2, replica_groups=mesh['face'=2,'tx'=4,'ty'=4] {'face'}, dimensions={0}, use_global_device_ids=true | all-gather | bytes 9216 | tf_op jit(solution)/shard_map/all_gather | solution.py:26
  8.5 1.3 collective-permute-start
  9.8 4.6 %collective-permute-start.1 = (f32[6,2,1,6,1,8]{5,4,3,1,2,0:T(1,128)S(1)}, f32[6,2,1,6,1,8]{5,4,3,1,2,0:T(1,128)S(1)}, u32[]{:S(2)}, u32[]{:S(2)}) collective-permute-start(f32[6,2,1,6,1,8]{5,4,3,1,2,0:T(1,128)S(1)} %get-tuple-element.67), channel_id=1, source_target_pairs={{0,4},{4,8},{8,12},{1,5},{5,9},{9,13},{2,6},{6,10},{10,14},{3,7},{... | collective-permute-start | bytes 6920 | tf_op jit(solution)/shard_map/ppermute | solution.py:18
  14.4 1.0 slice_reduce_fusion.7
  15.4 0.6 compare_reduce_fusion.3
  16.3 0.6 broadcast_multiply_fusion
  16.9 0.6 broadcast_multiply_fusion.2
  17.5 0.6 broadcast_multiply_fusion.3
  18.1 0.5 copy.1128
  18.6 0.5 copy.1127
  19.4 15.6 %all_gather.20 = f32[6,2,1,6,2,32]{3,4,2,1,0,5:T(2,128)S(1)} all-gather(f32[6,2,1,6,2,8]{3,4,2,1,0,5:T(2,128)S(1)} %copy.1129), channel_id=1, replica_groups=mesh['face'=2,'tx'=4,'ty'=4] {'tx'}, dimensions={5}, use_global_device_ids=true | all-gather | bytes 23040 | tf_op jit(solution)/shard_map/all_gather | solution.py:90
  35.1 0.3 copy.1130
  35.3 10.9 %psum.29 = f32[6,2,1,6,2,32]{5,1,4,3,0,2:T(2,128)S(1)} all-reduce(f32[6,2,1,6,2,32]{5,1,4,3,0,2:T(2,128)S(1)} %copy.1130), channel_id=1, replica_groups=mesh['face'=2,'tx'=4,'ty'=4] {'ty'}, use_global_device_ids=true, to_apply=%region_1.2 | all-reduce | flops 4608 | bytes 36864 | tf_op jit(solution)/shard_map/psum | solution.py:90
  46.6 6.8 %all_gather.19 = f32[6,2,1,6,2,32]{3,4,2,1,0,5:T(2,128)S(1)} all-gather(f32[6,2,1,6,2,8]{3,4,2,1,0,5:T(2,128)S(1)} %copy.1125), channel_id=1, replica_groups=mesh['face'=2,'tx'=4,'ty'=4] {'ty'}, dimensions={5}, use_global_device_ids=true | all-gather | bytes 23040 | tf_op jit(solution)/shard_map/all_gather | solution.py:89
  53.4 0.3 copy.1126
  53.6 18.5 %psum.28 = f32[6,2,1,6,2,32]{5,1,4,3,0,2:T(2,128)S(1)} all-reduce(f32[6,2,1,6,2,32]{5,1,4,3,0,2:T(2,128)S(1)} %copy.1126), channel_id=1, replica_groups=mesh['face'=2,'tx'=4,'ty'=4] {'tx'}, use_global_device_ids=true, to_apply=%region_0.0 | all-reduce | flops 4608 | bytes 36864 | tf_op jit(solution)/shard_map/psum | solution.py:89
  72.2 0.6 gather_fusion.3
  73.6 0.6 gather_fusion.2
  75.2 0.6 gather_fusion.1
  76.5 0.6 gather_fusion
  78.1 0.6 copy-done.20
  79.2 0.5 copy.1136
  79.7 1.3 collective-permute-start.3
  81.0 0.5 copy.1134
  81.6 1.3 collective-permute-start.2
  83.1 0.6 copy.1137
  83.6 2.4 %collective-permute-done.2 = f32[6,2,1,6,10,1]{4,1,5,3,2,0:T(2,128)S(1)} collective-permute-done((f32[6,2,1,6,10,1]{4,1,5,3,2,0:T(2,128)S(1)}, f32[6,2,1,6,10,1]{4,1,5,3,2,0:T(2,128)S(1)}, u32[]{:S(2)}, u32[]{:S(2)}) %collective-permute-start.2) | collective-permute-done | bytes 2912 | tf_op jit(solution)/shard_map/ppermute | solution.py:19
  86.1 0.6 copy.1135
  86.6 0.6 fusion.11
  87.8 0.7 copy.1145
  88.5 0.7 copy.1144
  89.2 14.9 %all_gather.22 = f32[9,2,1,6,2,32]{0,4,3,2,1,5:T(2,128)S(1)} all-gather(f32[9,2,1,6,2,8]{0,4,3,2,1,5:T(2,128)S(1)} %copy.1146), channel_id=1, replica_groups=mesh['face'=2,'tx'=4,'ty'=4] {'tx'}, dimensions={5}, use_global_device_ids=true | all-gather | bytes 34560 | tf_op jit(solution)/shard_map/all_gather | solution.py:90
  104.3 11.7 %psum.31 = f32[9,2,1,6,2,32]{5,1,4,3,0,2:T(2,128)S(1)} all-reduce(f32[9,2,1,6,2,32]{5,1,4,3,0,2:T(2,128)S(1)} %copy.1147), channel_id=1, replica_groups=mesh['face'=2,'tx'=4,'ty'=4] {'ty'}, use_global_device_ids=true, to_apply=%region_3.4 | all-reduce | flops 6912 | bytes 55296 | tf_op jit(solution)/shard_map/psum | solution.py:90
  116.4 6.8 %all_gather.21 = f32[9,2,1,6,2,32]{0,4,3,2,1,5:T(2,128)S(1)} all-gather(f32[9,2,1,6,2,8]{0,4,3,2,1,5:T(2,128)S(1)} %copy.1142), channel_id=1, replica_groups=mesh['face'=2,'tx'=4,'ty'=4] {'ty'}, dimensions={5}, use_global_device_ids=true | all-gather | bytes 34560 | tf_op jit(solution)/shard_map/all_gather | solution.py:89
  123.4 18.0 %psum.30 = f32[9,2,1,6,2,32]{5,1,4,3,0,2:T(2,128)S(1)} all-reduce(f32[9,2,1,6,2,32]{5,1,4,3,0,2:T(2,128)S(1)} %copy.1143), channel_id=1, replica_groups=mesh['face'=2,'tx'=4,'ty'=4] {'tx'}, use_global_device_ids=true, to_apply=%region_2.3 | all-reduce | flops 6912 | bytes 55296 | tf_op jit(solution)/shard_map/psum | solution.py:89
  141.6 0.7 gather_fusion.7
  142.3 0.7 gather_fusion.6
  142.9 0.7 gather_fusion.5
  143.6 0.7 gather_fusion.4
  144.2 1.3 collective-permute-start.4
  145.5 4.5 %collective-permute-start.5 = (f32[9,2,1,6,1,8]{5,4,3,1,2,0:T(1,128)S(1)}, f32[9,2,1,6,1,8]{5,4,3,1,2,0:T(1,128)S(1)}, u32[]{:S(2)}, u32[]{:S(2)}) collective-permute-start(f32[9,2,1,6,1,8]{5,4,3,1,2,0:T(1,128)S(1)} %get-tuple-element.61), channel_id=1, source_target_pairs={{0,4},{4,8},{8,12},{1,5},{5,9},{9,13},{2,6},{6,10},{10,14},{3,7},{... | collective-permute-start | bytes 10376 | tf_op jit(solution)/shard_map/ppermute | solution.py:18
  154.8 0.6 copy.1155
  155.4 0.6 copy.1154
  156.0 0.6 copy.1149
  156.7 0.6 copy.1148
  157.5 0.4 copy-done.1
  157.9 0.3 fusion.87
  158.2 1.3 copy.1152
  159.6 1.3 collective-permute-start.7
  160.9 0.8 copy.1150
  161.7 1.3 collective-permute-start.6
  163.0 0.3 fusion.7
  163.3 0.8 copy.1153
  164.1 2.3 %collective-permute-done.6 = f32[9,2,1,6,10,1]{4,1,5,3,2,0:T(2,128)} collective-permute-done((f32[9,2,1,6,10,1]{4,1,5,3,2,0:T(2,128)S(1)}, f32[9,2,1,6,10,1]{4,1,5,3,2,0:T(2,128)}, u32[]{:S(2)}, u32[]{:S(2)}) %collective-permute-start.6) | collective-permute-done | bytes 4352 | tf_op jit(solution)/shard_map/ppermute | solution.py:19
  166.3 1.6 copy.1151
  167.9 1.9 %fusion.3 = f32[9,2,1,6,8,8]{5,4,3,1,2,0:T(8,128)S(1)} fusion(f32[9,2,1,6,10,1]{5,4,3,1,2,0:T(8,128)S(1)} %copy.1153, f32[9,2,1,6,1,8]{5,4,3,1,2,0:T(1,128)S(1)} %collective-permute-done.4, f32[9,2,1,6,8,8]{5,4,3,1,2,0:T(8,128)S(1)} %constant_dynamic-update-slice_fusion.26, f32[9,2,1,6,1,8]{5,4,3,1,2,0:T(1,128)} %copy-done.1, ...), kind=kLoop, calls=%fused_computation.14 | loop fusion | flops 82944 | bytes 77776 | tf_op jit(solution)/shard_map/sub | solution.py:127
  169.8 0.7 copy-done.10
  170.6 4.9 %all_gather.23 = f32[2,2,6,8,8]{4,3,2,1,0:T(8,128)S(1)} all-gather(f32[1,2,6,8,8]{4,3,2,1,0:T(8,128)S(1)} %bitcast_multiply_fusion.2), channel_id=1, replica_groups=mesh['face'=2,'tx'=4,'ty'=4] {'face'}, dimensions={0}, use_global_device_ids=true | all-gather | bytes 9216 | tf_op jit(solution)/shard_map/all_gather | solution.py:26
  175.6 0.6 copy-done.7
  176.3 0.9 copy-done
  177.3 0.7 copy.1157
  (198 shorter events, 11.4 us)
Async XLA Ops:
  1.0 0.8 copy-start.16
  1.8 0.7 copy-start.11
  2.6 5.7 %copy-start.21 = (f32[1,6,8,8]{3,2,1,0:T(8,128)S(1)}, f32[1,6,8,8]{3,2,1,0:T(8,128)}, u32[]{:S(2)}) copy-start(f32[1,6,8,8]{3,2,1,0:T(8,128)} %param.10) | copy-start | bytes 4612
  8.4 6.1 %copy-start.17 = (s32[6,4,7]{2,1,0:T(4,128)S(1)}, s32[6,4,7]{2,1,0:T(4,128)}, u32[]{:S(2)}) copy-start(s32[6,4,7]{2,1,0:T(4,128)} %param.13) | copy-start | bytes 2020
  8.5 70.3 %collective-permute-start = (f32[6,2,1,6,1,8]{5,4,3,1,2,0:T(1,128)S(1)}, f32[6,2,1,6,1,8]{5,4,3,1,2,0:T(1,128)S(1)}, u32[]{:S(2)}, u32[]{:S(2)}) collective-permute-start(f32[6,2,1,6,1,8]{5,4,3,1,2,0:T(1,128)S(1)} %get-tuple-element.68), channel_id=1, source_target_pairs={{4,0},{8,4},{12,8},{5,1},{9,5},{13,9},{6,2},{10,6},{14,10},{7,3},{... | collective-permute-start | bytes 6920 | tf_op jit(solution)/shard_map/ppermute | solution.py:19
  9.8 69.0 %collective-permute-start.1 = (f32[6,2,1,6,1,8]{5,4,3,1,2,0:T(1,128)S(1)}, f32[6,2,1,6,1,8]{5,4,3,1,2,0:T(1,128)S(1)}, u32[]{:S(2)}, u32[]{:S(2)}) collective-permute-start(f32[6,2,1,6,1,8]{5,4,3,1,2,0:T(1,128)S(1)} %get-tuple-element.67), channel_id=1, source_target_pairs={{0,4},{4,8},{8,12},{1,5},{5,9},{9,13},{2,6},{6,10},{10,14},{3,7},{... | collective-permute-start | bytes 6920 | tf_op jit(solution)/shard_map/ppermute | solution.py:18
  16.3 70.3 %copy-start.25 = (pred[8]{0:T(512)(128)(4,1)}, pred[8]{0:T(512)(128)(4,1)S(1)}, u32[]{:S(2)}) copy-start(pred[8]{0:T(512)(128)(4,1)S(1)} %compare_and_fusion.2) | copy-start | bytes 28
  77.8 0.9 copy-start.20
  78.7 8.6 %copy-start.14 = (f32[6,8,8]{2,1,0:T(8,128)}, f32[6,8,8]{2,1,0:T(8,128)S(1)}, u32[]{:S(2)}) copy-start(f32[6,8,8]{2,1,0:T(8,128)S(1)} %get-tuple-element.73) | copy-start | bytes 4612
  78.7 8.6 %copy-start.12 = (f32[6,8,8]{2,1,0:T(8,128)}, f32[6,8,8]{2,1,0:T(8,128)S(1)}, u32[]{:S(2)}) copy-start(f32[6,8,8]{2,1,0:T(8,128)S(1)} %get-tuple-element.72) | copy-start | bytes 4612
  78.7 8.7 %copy-start.6 = (f32[6,8,8]{2,1,0:T(8,128)}, f32[6,8,8]{2,1,0:T(8,128)S(1)}, u32[]{:S(2)}) copy-start(f32[6,8,8]{2,1,0:T(8,128)S(1)} %get-tuple-element.74) | copy-start | bytes 4612
  78.7 8.7 %copy-start.8 = (f32[6,8,8]{2,1,0:T(8,128)}, f32[6,8,8]{2,1,0:T(8,128)S(1)}, u32[]{:S(2)}) copy-start(f32[6,8,8]{2,1,0:T(8,128)S(1)} %get-tuple-element.71) | copy-start | bytes 4612
  78.7 4.1 %copy-start.23 = (pred[8]{0:T(512)(128)(4,1)}, pred[8]{0:T(512)(128)(4,1)S(1)}, u32[]{:S(2)}) copy-start(pred[8]{0:T(512)(128)(4,1)S(1)} %compare_and_fusion.3) | copy-start | bytes 28
  79.7 3.3 %collective-permute-start.3 = (f32[6,2,1,6,10,1]{4,1,5,3,2,0:T(2,128)S(1)}, f32[6,2,1,6,10,1]{4,1,5,3,2,0:T(2,128)S(1)}, u32[]{:S(2)}, u32[]{:S(2)}) collective-permute-start(f32[6,2,1,6,10,1]{4,1,5,3,2,0:T(2,128)S(1)} %copy.1136), channel_id=1, source_target_pairs={{0,1},{1,2},{2,3},{4,5},{5,6},{6,7},{8,9},{9,10},{10,11},{12,13},{... | collective-permute-start | bytes 8648 | tf_op jit(solution)/shard_map/ppermute | solution.py:18
  81.6 4.5 %collective-permute-start.2 = (f32[6,2,1,6,10,1]{4,1,5,3,2,0:T(2,128)S(1)}, f32[6,2,1,6,10,1]{4,1,5,3,2,0:T(2,128)S(1)}, u32[]{:S(2)}, u32[]{:S(2)}) collective-permute-start(f32[6,2,1,6,10,1]{4,1,5,3,2,0:T(2,128)S(1)} %copy.1134), channel_id=1, source_target_pairs={{1,0},{2,1},{3,2},{5,4},{6,5},{7,6},{9,8},{10,9},{11,10},{13,12},{... | collective-permute-start | bytes 8648 | tf_op jit(solution)/shard_map/ppermute | solution.py:19
  144.2 13.1 %collective-permute-start.4 = (f32[9,2,1,6,1,8]{5,4,3,1,2,0:T(1,128)S(1)}, f32[9,2,1,6,1,8]{5,4,3,1,2,0:T(1,128)S(1)}, u32[]{:S(2)}, u32[]{:S(2)}) collective-permute-start(f32[9,2,1,6,1,8]{5,4,3,1,2,0:T(1,128)S(1)} %get-tuple-element.62), channel_id=1, source_target_pairs={{4,0},{8,4},{12,8},{5,1},{9,5},{13,9},{6,2},{10,6},{14,10},{7,3},{... | collective-permute-start | bytes 10376 | tf_op jit(solution)/shard_map/ppermute | solution.py:19
  145.5 11.8 %collective-permute-start.5 = (f32[9,2,1,6,1,8]{5,4,3,1,2,0:T(1,128)S(1)}, f32[9,2,1,6,1,8]{5,4,3,1,2,0:T(1,128)S(1)}, u32[]{:S(2)}, u32[]{:S(2)}) collective-permute-start(f32[9,2,1,6,1,8]{5,4,3,1,2,0:T(1,128)S(1)} %get-tuple-element.61), channel_id=1, source_target_pairs={{0,4},{4,8},{8,12},{1,5},{5,9},{9,13},{2,6},{6,10},{10,14},{3,7},{... | collective-permute-start | bytes 10376 | tf_op jit(solution)/shard_map/ppermute | solution.py:18
  157.3 0.6 copy-start.1
  159.6 3.7 %collective-permute-start.7 = (f32[9,2,1,6,10,1]{4,1,5,3,2,0:T(2,128)}, f32[9,2,1,6,10,1]{4,1,5,3,2,0:T(2,128)S(1)}, u32[]{:S(2)}, u32[]{:S(2)}) collective-permute-start(f32[9,2,1,6,10,1]{4,1,5,3,2,0:T(2,128)} %copy.1152), channel_id=1, source_target_pairs={{0,1},{1,2},{2,3},{4,5},{5,6},{6,7},{8,9},{9,10},{10,11},{12,13},{... | collective-permute-start | bytes 12968 | tf_op jit(solution)/shard_map/ppermute | solution.py:18
  160.9 2.1 %copy-start.2 = (f32[9,2,1,6,1,8]{5,4,3,1,2,0:T(1,128)S(1)}, f32[9,2,1,6,1,8]{5,4,3,1,2,0:T(1,128)}, u32[]{:S(2)}) copy-start(f32[9,2,1,6,1,8]{5,4,3,1,2,0:T(1,128)} %copy-done.1) | copy-start | bytes 10372
  160.9 2.1 %copy-start.4 = (f32[9,2,6,8]{3,2,1,0:T(8,128)S(1)}, f32[9,2,6,8]{3,2,1,0:T(8,128)}, u32[]{:S(2)}) copy-start(f32[9,2,6,8]{3,2,1,0:T(8,128)} %copy.1149) | copy-start | bytes 10372
  160.9 2.1 %copy-start.5 = (f32[9,2,6,8]{3,2,1,0:T(8,128)S(1)}, f32[9,2,6,8]{3,2,1,0:T(8,128)}, u32[]{:S(2)}) copy-start(f32[9,2,6,8]{3,2,1,0:T(8,128)} %copy.1148) | copy-start | bytes 10372
  160.9 2.1 %copy-start.24 = (pred[8]{0:T(512)(128)(4,1)S(1)}, pred[8]{0:T(512)(128)(4,1)}, u32[]{:S(2)}) copy-start(pred[8]{0:T(512)(128)(4,1)} %copy-done.23) | copy-start | bytes 28
  161.7 4.7 %collective-permute-start.6 = (f32[9,2,1,6,10,1]{4,1,5,3,2,0:T(2,128)S(1)}, f32[9,2,1,6,10,1]{4,1,5,3,2,0:T(2,128)}, u32[]{:S(2)}, u32[]{:S(2)}) collective-permute-start(f32[9,2,1,6,10,1]{4,1,5,3,2,0:T(2,128)S(1)} %copy.1150), channel_id=1, source_target_pairs={{1,0},{2,1},{3,2},{5,4},{6,5},{7,6},{9,8},{10,9},{11,10},{13,12},{... | collective-permute-start | bytes 12968 | tf_op jit(solution)/shard_map/ppermute | solution.py:19
  164.1 3.8 %copy-start.26 = (pred[8]{0:T(512)(128)(4,1)S(1)}, pred[8]{0:T(512)(128)(4,1)}, u32[]{:S(2)}) copy-start(pred[8]{0:T(512)(128)(4,1)} %copy-done.25) | copy-start | bytes 28
  167.9 1.9 %copy-start.9 = (f32[6,8,8]{2,1,0:T(8,128)S(1)}, f32[6,8,8]{2,1,0:T(8,128)}, u32[]{:S(2)}) copy-start(f32[6,8,8]{2,1,0:T(8,128)} %copy-done.8) | copy-start | bytes 4612
  169.8 0.7 copy-start.10
  170.5 4.9 %copy-start.13 = (f32[6,8,8]{2,1,0:T(8,128)S(1)}, f32[6,8,8]{2,1,0:T(8,128)}, u32[]{:S(2)}) copy-start(f32[6,8,8]{2,1,0:T(8,128)} %copy-done.12) | copy-start | bytes 4612
  170.6 4.9 %copy-start.15 = (f32[6,8,8]{2,1,0:T(8,128)S(1)}, f32[6,8,8]{2,1,0:T(8,128)}, u32[]{:S(2)}) copy-start(f32[6,8,8]{2,1,0:T(8,128)} %copy-done.14) | copy-start | bytes 4612
  170.6 4.9 %copy-start.22 = (f32[6,8,8]{2,1,0:T(8,128)S(1)}, f32[6,8,8]{2,1,0:T(8,128)}, u32[]{:S(2)}) copy-start(f32[6,8,8]{2,1,0:T(8,128)} %broadcast_multiply_fusion.3) | copy-start | bytes 4612
  175.5 0.7 copy-start.7
  175.5 0.7 copy-start.18
  175.5 0.8 copy-start.19
  176.2 0.9 copy-start
  176.2 1.0 copy-start.3
where the time goes:
time: 180 us; the launch traced here: 178 us
  blocking collectives  114 us (63%)
  local copies, waits for them, and re-layouts  27.4 us (15%)
  starting transfers between devices  16.9 us (9%)
  other arithmetic  14 us (8%)
  waiting for transfers between devices  4.71 us (3%)
    psum x2, blocking collectives, face_rows(): lax.psum(lax.all_gather(row_pair, 'ty', axis=5, tiled=True), 'tx')  36.5 us
    all_gather x2, blocking collectives, face_rows(): lax.all_gather(column_pair, 'tx', axis=5, tiled=True)  30.5 us
    psum x2, blocking collectives, face_rows(): lax.psum(lax.all_gather(column_pair, 'tx', axis=5, tiled=True), 'ty')  22.6 us
    all_gather x2, blocking collectives, face_rows(): lax.all_gather(row_pair, 'ty', axis=5, tiled=True)  13.6 us
    ppermute x4, starting transfers between devices, padded_2(): before = lax.ppermute(last, axis, up)  11.7 us
    all_gather x2, blocking collectives, carried_in(): pieces = lax.all_gather(value, axis)  10.6 us
    unnamed x75, local copies, waits for them, and re-layouts  6.54 us
    gather x8, local copies, waits for them, and re-layouts, orient(): chosen = edge_rows[:, :, :, source_face, source_edge, :]  5.17 us
  transfers between devices with their start and end apart: 8, of which 2 were waited for; matrix products, arithmetic and copies ran while one was open for 12% of the time, Pallas kernels for 0%

commit v1 on v0

--- a/solution.py
+++ b/solution.py
@@ -1,7 +1,15 @@
+import functools
+
 import jax
 import jax.numpy as jnp
 from jax import lax
+from jax.experimental import pallas as pl
+from jax.experimental.pallas import tpu as pltpu
 from jax.sharding import PartitionSpec as P
+
+MESH = pl.DeviceIdType.MESH
+SUBLANES = 8
+LANES = 128
 
 time_increment = 0.3
 forward_layout = (("vector", 0), ("vector", 2), ("scalar", 4), ("scalar", 5))
@@ -245,9 +253,477 @@
     return probes + spread[None] * adjoint_out
 
 
+def rolled(tile, shift, axis):
+    return pltpu.roll(tile, shift % tile.shape[axis], axis)
+
+
+def block_transposed(tile, sub, inner):
+    step = SUBLANES // 2
+    while step:
+        ahead = rolled(rolled(tile, -step, 0), step, 1)
+        behind = rolled(rolled(tile, step, 0), -step, 1)
+        low_row = (sub & step) == 0
+        low_lane = (inner & step) == 0
+        tile = jnp.where(low_row == low_lane, tile, jnp.where(low_row, ahead, behind))
+        step //= 2
+    return tile
+
+
+def block_reversed(tile, inner):
+    step = SUBLANES // 2
+    while step:
+        tile = jnp.where(
+            (inner & step) == 0, rolled(tile, -step, 1), rolled(tile, step, 1)
+        )
+        step //= 2
+    return tile
+
+
+def tile_kernel(
+    count,
+    faces,
+    probes_ref,
+    wind_ref,
+    mass_ref,
+    heat_ref,
+    spread_ref,
+    variance_ref,
+    links_ref,
+    out_ref,
+    strips_f,
+    strips_a,
+    halo_f,
+    halo_a,
+    slots_f,
+    slots_a,
+    below_ref,
+    above_ref,
+    column_f,
+    column_a,
+    send_f,
+    send_a,
+    recv_halo_f,
+    recv_halo_a,
+    recv_slot_f,
+    recv_slot_a,
+    send_below,
+    send_above,
+    recv_below,
+    recv_above,
+):
+    level = lax.axis_index("face")
+    row = lax.axis_index("tx")
+    column = lax.axis_index("ty")
+    probe_count = probes_ref.shape[0]
+    panels = probes_ref.shape[3]
+    last = count - 1
+    at = [row == 0, row == last, column == 0, column == last]
+    on_row = at[0] | at[1]
+    on_column = at[2] | at[3]
+    corner = on_row & on_column
+    middle = (on_row | on_column) & ~corner
+    row_edge = jnp.where(at[0], 0, 1)
+    column_edge = jnp.where(at[2], 2, 3)
+    half = count // 2
+    row_part = jnp.where(column < half, 0, 1)
+    column_part = jnp.where(row < half, 0, 1)
+    row_slot = row_edge * 2 + row_part
+    column_slot = column_edge * 2 + column_part
+    own_edge = jnp.where(on_row, row_edge, column_edge)
+    own_slot = jnp.where(on_row, row_slot, column_slot)
+    along = jnp.where(on_row, column, row)
+    near = jnp.where(along < half, along, last - along)
+
+    def slot_place(edge, part):
+        segment = near if part == 0 else last - near
+        return [(0, segment), (last, segment), (segment, 0), (segment, last)][edge]
+
+    beside = [(row - 1, column), (row + 1, column), (row, column - 1), (row, column + 1)]
+    corners = [(0, 0), (0, last), (last, 0), (last, last)]
+
+    barrier = pltpu.get_barrier_semaphore()
+
+    def greet(place):
+        pl.semaphore_signal(
+            barrier,
+            inc=1,
+            device_id={"tx": place[0], "ty": place[1]},
+            device_id_type=MESH,
+        )
+
+    for d in range(4):
+        @pl.when(~at[d])
+        def _():
+            greet(beside[d])
+
+    @pl.when(middle)
+    def _():
+        for slot in range(8):
+            @pl.when(own_slot != slot)
+            def _():
+                greet(slot_place(slot // 2, slot % 2))
+
+    @pl.when(corner)
+    def _():
+        for place in corners:
+            @pl.when((row != place[0]) | (column != place[1]))
+            def _():
+                greet(place)
+
+    for other in range(faces):
+        @pl.when(level != other)
+        def _():
+            pl.semaphore_signal(
+                barrier, inc=1, device_id={"face": other}, device_id_type=MESH
+            )
+
+    expected = faces - 1 + jnp.where(middle, 7, 0) + jnp.where(corner, 3, 0)
+    for d in range(4):
+        expected = expected + jnp.where(at[d], 0, 1)
+
+    sub = lax.broadcasted_iota(jnp.int32, (SUBLANES, LANES), 0)
+    lane = lax.broadcasted_iota(jnp.int32, (SUBLANES, LANES), 1)
+    inner = lane % SUBLANES
+    panel_of = (lane // SUBLANES) % panels
+
+    def packed(tiles):
+        width = LANES - SUBLANES * len(tiles)
+        return jnp.concatenate(tiles + [jnp.zeros((SUBLANES, width), jnp.float32)], axis=1)
+
+    def per_panel(load):
+        return packed([load(f) for f in range(panels)] * probe_count)
+
+    def per_probe(component):
+        return packed(
+            [
+                probes_ref[p, component, 0, f]
+                for p in range(probe_count)
+                for f in range(panels)
+            ]
+        )
+
+    def level_copy(other, source, target, send, recv):
+        return pltpu.make_async_remote_copy(
+            src_ref=source,
+            dst_ref=target,
+            send_sem=send,
+            recv_sem=recv,
+            device_id={"face": other},
+            device_id_type=MESH,
+        )
+
+    def below_copy(other, slot):
+        return level_copy(
+            other, column_f, below_ref.at[slot], send_below.at[other], recv_below.at[slot]
+        )
+
+    def above_copy(other, slot):
+        return level_copy(
+            other, column_a, above_ref.at[slot], send_above.at[other], recv_above.at[slot]
+        )
+
+    probe_h = per_probe(2)
+    spread_h = per_panel(lambda f: spread_ref[2, 0, f])
+    h = spread_h * probe_h
+    column_f[...] = h
+    pl.semaphore_wait(barrier, expected)
+    for other in range(1, faces):
+        @pl.when(level < other)
+        def _():
+            below_copy(other, level).start()
+
+    probe_z, probe_m, probe_t = per_probe(0), per_probe(1), per_probe(3)
+    spread_z, spread_m, spread_t = [
+        per_panel(lambda f, c=c: spread_ref[c, 0, f]) for c in (0, 1, 3)
+    ]
+    u, v = [per_panel(lambda f, c=c: wind_ref[c, 0, f]) for c in range(2)]
+    mass = per_panel(lambda f: mass_ref[0, f])
+    heat = per_panel(lambda f: heat_ref[0, f])
+    z, m, t = spread_z * probe_z, spread_m * probe_m, spread_t * probe_t
+    fx = u * h + mass * z
+    fy = v * h + mass * m
+
+    def write_strips(strips, x_fields, y_fields):
+        low = jnp.zeros((SUBLANES, LANES), jnp.float32)
+        high = low
+        for c, field in enumerate(x_fields):
+            low = jnp.where(sub == c, field[0:1, :], low)
+            high = jnp.where(sub == c, field[SUBLANES - 1 : SUBLANES, :], high)
+        strips[0] = low
+        strips[1] = high
+        low = jnp.zeros((SUBLANES, LANES), jnp.float32)
+        high = low
+        for c, field in enumerate(y_fields):
+            low = jnp.where(inner == c, rolled(field, c, 1), low)
+            high = jnp.where(inner == c, rolled(field, c - (SUBLANES - 1), 1), high)
+        strips[2] = block_transposed(low, sub, inner)
+        strips[3] = block_transposed(high, sub, inner)
+
+    def strip_copy(source, target, send, recv, place):
+        return pltpu.make_async_remote_copy(
+            src_ref=source,
+            dst_ref=target,
+            send_sem=send,
+            recv_sem=recv,
+            device_id={"tx": place[0], "ty": place[1]},
+            device_id_type=MESH,
+        )
+
+    def each_send(strips, halo, slots, send, recv_halo, recv_slot, act):
+        @pl.when(middle)
+        def _():
+            for slot in range(8):
+                @pl.when(own_slot != slot)
+                def _():
+                    act(
+                        strip_copy(
+                            strips.at[own_edge],
+                            slots.at[own_slot],
+                            send.at[4 + slot],
+                            recv_slot.at[own_slot],
+                            slot_place(slot // 2, slot % 2),
+                        )
+                    )
+
+        @pl.when(corner)
+        def _():
+            for number, place in enumerate(corners):
+                @pl.when((row != place[0]) | (column != place[1]))
+                def _():
+                    for kind, (edge, slot) in enumerate(
+                        ((row_edge, row_slot), (column_edge, column_slot))
+                    ):
+                        act(
+                            strip_copy(
+                                strips.at[edge],
+                                slots.at[slot],
+                                send.at[4 + number * 2 + kind],
+                                recv_slot.at[slot],
+                                place,
+                            )
+                        )
+
+        for d in range(4):
+            @pl.when(~at[d])
+            def _():
+                act(
+                    strip_copy(
+                        strips.at[d],
+                        halo.at[d ^ 1],
+                        send.at[d],
+                        recv_halo.at[d ^ 1],
+                        beside[d],
+                    )
+                )
+
+    def ghost_across(slots, edge, part, is_row, is_adjoint):
+        strip = jnp.zeros((SUBLANES, LANES), jnp.float32)
+        reverse = jnp.zeros((SUBLANES, LANES), jnp.int32)
+        entries = [strip] * 4
+        for f in range(panels):
+            source = links_ref[f, edge, 0]
+            flip = links_ref[f, edge, 2]
+            slot = links_ref[f, edge, 1] * 2 + jnp.where(flip == 1, 1 - part, part)
+            shift = (SUBLANES * (f - source) + LANES) % LANES
+            here = panel_of == f
+            strip = jnp.where(here, pltpu.roll(slots[slot], shift, 1), strip)
+            reverse = jnp.where(here, flip, reverse)
+            entries = [
+                jnp.where(here, links_ref[f, edge, 3 + i].astype(jnp.float32), entries[i])
+                for i in range(4)
+            ]
+        strip = jnp.where(reverse == 1, block_reversed(strip, inner), strip)
+        m0, m1, m2, m3 = entries
+        normal = m0 + m1 if is_row else m2 + m3
+        first = m0 * strip + m1 * rolled(strip, -1, 0)
+        second = m3 * strip + m2 * rolled(strip, 1, 0)
+        if is_adjoint:
+            vectors = jnp.where(sub == 0, first, second) * normal
+            return jnp.where(
+                sub < 2, vectors, jnp.where(sub == 3, strip, normal * strip)
+            )
+        vectors = jnp.where(sub == 0, first, second)
+        return jnp.where(sub < 2, vectors, jnp.where(sub == 2, normal * strip, strip))
+
+    def receive(strips, halo, slots, send, recv_halo, recv_slot, is_adjoint):
+        def arrival(target, semaphore):
+            strip_copy(strips.at[0], target, send.at[0], semaphore, (row, column)).wait_recv()
+
+        for d in range(4):
+            @pl.when(~at[d])
+            def _():
+                arrival(halo.at[d], recv_halo.at[d])
+
+        @pl.when(on_row)
+        def _():
+            slots[row_slot] = strips[row_edge]
+
+        @pl.when(on_column)
+        def _():
+            slots[column_slot] = strips[column_edge]
+
+        @pl.when(on_row | on_column)
+        def _():
+            for slot in range(8):
+                mine = (on_row & (row_slot == slot)) | (on_column & (column_slot == slot))
+
+                @pl.when(~mine)
+                def _():
+                    arrival(slots.at[slot], recv_slot.at[slot])
+
+        @pl.when(on_row)
+        def _():
+            halo[row_edge] = ghost_across(slots, row_edge, row_part, True, is_adjoint)
+
+        @pl.when(on_column)
+        def _():
+            halo[column_edge] = ghost_across(
+                slots, column_edge, column_part, False, is_adjoint
+            )
+
+    def slopes_of(halo, x_fields, y_fields):
+        low, high = halo[0], halo[1]
+        east = []
+        for c, field in enumerate(x_fields):
+            before = jnp.where(sub == 0, low[c : c + 1, :], rolled(field, 1, 0))
+            after = jnp.where(sub == SUBLANES - 1, high[c : c + 1, :], rolled(field, -1, 0))
+            east.append(0.5 * (after - before))
+        low = block_transposed(halo[2], sub, inner)
+        high = block_transposed(halo[3], sub, inner)
+        north = []
+        for c, field in enumerate(y_fields):
+            before = jnp.where(inner == 0, rolled(low, -c, 1), rolled(field, 1, 1))
+            after = jnp.where(
+                inner == SUBLANES - 1, rolled(high, SUBLANES - 1 - c, 1), rolled(field, -1, 1)
+            )
+            north.append(0.5 * (after - before))
+        return east, north
+
+    forward = (strips_f, halo_f, slots_f, send_f, recv_halo_f, recv_slot_f)
+    adjoint = (strips_a, halo_a, slots_a, send_a, recv_halo_a, recv_slot_a)
+
+    for other in range(faces):
+        @pl.when(level <= other)
+        def _():
+            below_ref[other] = jnp.zeros((SUBLANES, LANES), jnp.float32)
+
+        @pl.when(level > other)
+        def _():
+            below_copy(other, other).wait_recv()
+
+    pressure = h
+    for other in range(faces):
+        pressure = pressure + below_ref[other]
+    geo = t + heat * pressure
+    x_fields, y_fields = (z, m, fx, t, geo), (z, m, fy, t, geo)
+    write_strips(strips_f, x_fields, y_fields)
+    each_send(*forward, lambda copy: copy.start())
+    var_z, var_m, var_h, var_t = [
+        per_panel(lambda f, c=c: variance_ref[c, 0, f]) for c in range(4)
+    ]
+    receive(*forward, False)
+    east, north = slopes_of(halo_f, x_fields, y_fields)
+    zc = var_z * (z - time_increment * (east[4] + u * east[0] + v * north[0]))
+    mc = var_m * (m - time_increment * (north[4] + u * east[1] + v * north[1]))
+    hc = var_h * (h - time_increment * (east[2] + north[2]))
+    tc = var_t * (t - time_increment * (u * east[3] + v * north[3]))
+
+    x_fields, y_fields = (u * zc, u * mc, zc, hc, u * tc), (v * zc, v * mc, mc, hc, v * tc)
+    write_strips(strips_a, x_fields, y_fields)
+    each_send(*adjoint, lambda copy: copy.start())
+    receive(*adjoint, True)
+    east, north = slopes_of(halo_a, x_fields, y_fields)
+    geo_back = time_increment * (east[2] + north[2])
+    load = heat * geo_back
+    column_a[...] = load
+    for other in range(faces):
+        @pl.when(level > other)
+        def _():
+            above_copy(other, level).start()
+
+    flux_east = time_increment * east[3]
+    flux_north = time_increment * north[3]
+    z_back = zc + time_increment * (east[0] + north[0]) + mass * flux_east
+    m_back = mc + time_increment * (east[1] + north[1]) + mass * flux_north
+    t_back = tc + time_increment * (east[4] + north[4]) + geo_back
+
+    def put(component, tile):
+        for p in range(probe_count):
+            for f in range(panels):
+                start = (p * panels + f) * SUBLANES
+                out_ref[p, component, 0, f] = tile[:, start : start + SUBLANES]
+
+    put(0, probe_z + spread_z * z_back)
+    put(1, probe_m + spread_m * m_back)
+    put(3, probe_t + spread_t * t_back)
+
+    for other in range(faces):
+        @pl.when(level >= other)
+        def _():
+            above_ref[other] = jnp.zeros((SUBLANES, LANES), jnp.float32)
+
+        @pl.when(level < other)
+        def _():
+            above_copy(other, other).wait_recv()
+
+    for other in range(faces):
+        load = load + above_ref[other]
+    put(2, probe_h + spread_h * (hc + u * flux_east + v * flux_north + load))
+
+    each_send(*forward, lambda copy: copy.wait_send())
+    each_send(*adjoint, lambda copy: copy.wait_send())
+    for other in range(faces):
+        @pl.when(level < other)
+        def _():
+            below_copy(other, level).wait_send()
+
+        @pl.when(level > other)
+        def _():
+            above_copy(other, level).wait_send()
+
+
+def fused(count, faces, *operands):
+    tile = (SUBLANES, LANES)
+    vmem = pl.BlockSpec(memory_space=pltpu.VMEM)
+    probes = operands[0]
+    strips = pltpu.VMEM((4, *tile), jnp.float32)
+    slots = pltpu.VMEM((8, *tile), jnp.float32)
+    levels = pltpu.VMEM((faces, *tile), jnp.float32)
+    one = pltpu.VMEM(tile, jnp.float32)
+    dma = pltpu.SemaphoreType.DMA
+    return pl.pallas_call(
+        functools.partial(tile_kernel, count, faces),
+        out_shape=jax.ShapeDtypeStruct(probes.shape, probes.dtype),
+        in_specs=[vmem] * 6 + [pl.BlockSpec(memory_space=pltpu.SMEM)],
+        out_specs=vmem,
+        scratch_shapes=[strips] * 4
+        + [slots] * 2
+        + [levels] * 2
+        + [one] * 2
+        + [dma((12,))] * 2
+        + [dma((4,))] * 2
+        + [dma((8,))] * 2
+        + [dma((faces,))] * 4,
+        compiler_params=pltpu.CompilerParams(collective_id=0, has_side_effects=True),
+    )(*operands)
+
+
 def solution(mesh):
+    count, faces = mesh.shape["tx"], mesh.shape["face"]
+
+    def chosen(*operands):
+        probe_count, _, levels, panels, rows, columns = operands[0].shape
+        fits = (
+            levels == 1
+            and count == mesh.shape["ty"]
+            and count % 2 == 0
+            and rows == columns == SUBLANES
+            and probe_count * panels * SUBLANES < LANES
+        )
+        return fused(count, faces, *operands) if fits else body(*operands)
+
     return jax.shard_map(
-        body,
+        chosen,
         mesh=mesh,
         in_specs=(
             P(None, None, "face", None, "tx", "ty"),

time: 180 us -> 24.5 us (0.14); the launches traced: 178 us -> 24.3 us
  blocking collectives: 114 us -> 0 us
  local copies, waits for them, and re-layouts: 27.4 us -> 1.62 us
  Pallas kernels: 0 us -> 22.7 us
  starting transfers between devices: 16.9 us -> 0 us
  other arithmetic: 14 us -> 0 us
  waiting for transfers between devices: 4.71 us -> 0 us
    psum x4 -> x0, blocking collectives: 59.1 us -> none  [the longest x2 36.5 us: face_rows(): lax.psum(lax.all_gather(row_pair, 'ty', axis=5, tiled=True), 'tx')]
    all_gather x6 -> x0, blocking collectives: 54.7 us -> none  [the longest x2 30.5 us: face_rows(): lax.all_gather(column_pair, 'tx', axis=5, tiled=True)]
    pallas_call x0 -> x1, Pallas kernels: none -> 22.7 us  [fused(): pl.pallas_call(functools.partial(tile_kernel, count, faces), out_shape=ja...]
    ppermute x8 -> x0, starting transfers between devices: 16.9 us -> none  [the longest x4 11.7 us: padded_2(): before = lax.ppermute(last, axis, up)]
    gather x8 -> x0, local copies, waits for them, and re-layouts: 5.17 us -> none  [orient(): chosen = edge_rows[:, :, :, source_face, source_edge, :]]
    unnamed x75 -> x1, local copies, waits for them, and re-layouts: 6.54 us -> 1.62 us
    slice x9 -> x0, local copies, waits for them, and re-layouts: 4.82 us -> none  [the longest x2 1.89 us: padded_2(): last = lax.slice_in_dim(array, length - width, length, axis=dim)]
    ppermute x8 -> x0, waiting for transfers between devices: 4.71 us -> none  [the longest x4 4.7 us: padded_2(): after = lax.ppermute(leading, axis, down)]
  transfers between devices with their start and end apart: 8 -> 0, of which waited for: 2 -> 0; matrix products, arithmetic and copies ran while one was open for 12% -> 0% of each run, Pallas kernels for 0% -> 0%
where the time goes in v1:
time: 24.5 us; the launch traced here: 24.3 us
  Pallas kernels  22.7 us (93%)
  local copies, waits for them, and re-layouts  1.62 us (7%)
    pallas_call x1, Pallas kernels, fused(): pl.pallas_call(functools.partial(tile_kernel, count, faces), out_shape=ja...  22.7 us
    unnamed x1, local copies, waits for them, and re-layouts  1.62 us

profile of v1, /device:TPU:0, one launch (start us, length us, event | category | flops | bytes accessed | tf_op | source)
XLA Modules:
  0.0 24.3 jit_solution(3911457954358307242)
XLA Ops:
  0.0 22.7 %shard_map.73 = f32[2,4,1,6,8,8]{5,4,3,2,1,0:T(8,128)} custom-call(f32[2,4,1,6,8,8]{5,4,3,2,1,0:T(8,128)} %probes_ref.1, f32[2,1,6,8,8]{4,3,2,1,0:T(8,128)} %wind_ref.1, f32[1,6,8,8]{3,2,1,0:T(8,128)} %mass_ref.1, f32[1,6,8,8]{3,2,1,0:T(8,128)} %heat_ref.1, f32[4,1,6,8,8]{4,3,2,1,0:T(8,128)} %spread_ref.1, f32[4,1,6,8,8]{4,3,2,1,0:T(8,128)} %variance_ref.1, ...), custom_call_target="tpu_custom_call" | custom-call | tf_op jit(solution)/shard_map/pallas_call | solution.py:694
  22.7 1.6 %copy.9 = f32[2,4,1,6,8,8]{5,4,3,2,1,0:T(8,128)} copy(f32[2,4,1,6,8,8]{5,4,3,2,1,0:T(8,128)} %shard_map.73) | data formatting | bytes 24576

commit v2 on v1

--- a/solution.py
+++ b/solution.py
@@ -282,6 +282,14 @@
 def tile_kernel(
     count,
     faces,
+    probes_hbm,
+    wind_hbm,
+    mass_hbm,
+    heat_hbm,
+    spread_hbm,
+    variance_hbm,
+    links_hbm,
+    out_hbm,
     probes_ref,
     wind_ref,
     mass_ref,
@@ -290,6 +298,8 @@
     variance_ref,
     links_ref,
     out_ref,
+    take_sem,
+    put_sem,
     strips_f,
     strips_a,
     halo_f,
@@ -377,6 +387,23 @@
                 barrier, inc=1, device_id={"face": other}, device_id_type=MESH
             )
 
+    taken = [
+        pltpu.make_async_copy(source, target, take_sem.at[i])
+        for i, (source, target) in enumerate(
+            (
+                (probes_hbm, probes_ref),
+                (spread_hbm, spread_ref),
+                (wind_hbm, wind_ref),
+                (mass_hbm, mass_ref),
+                (heat_hbm, heat_ref),
+                (variance_hbm, variance_ref),
+                (links_hbm, links_ref),
+            )
+        )
+    ]
+    for copy in taken:
+        copy.start()
+
     expected = faces - 1 + jnp.where(middle, 7, 0) + jnp.where(corner, 3, 0)
     for d in range(4):
         expected = expected + jnp.where(at[d], 0, 1)
@@ -422,6 +449,8 @@
             other, column_a, above_ref.at[slot], send_above.at[other], recv_above.at[slot]
         )
 
+    for copy in taken[:2]:
+        copy.wait()
     probe_h = per_probe(2)
     spread_h = per_panel(lambda f: spread_ref[2, 0, f])
     h = spread_h * probe_h
@@ -436,6 +465,8 @@
     spread_z, spread_m, spread_t = [
         per_panel(lambda f, c=c: spread_ref[c, 0, f]) for c in (0, 1, 3)
     ]
+    for copy in taken[2:5]:
+        copy.wait()
     u, v = [per_panel(lambda f, c=c: wind_ref[c, 0, f]) for c in range(2)]
     mass = per_panel(lambda f: mass_ref[0, f])
     heat = per_panel(lambda f: heat_ref[0, f])
@@ -618,6 +649,8 @@
     x_fields, y_fields = (z, m, fx, t, geo), (z, m, fy, t, geo)
     write_strips(strips_f, x_fields, y_fields)
     each_send(*forward, lambda copy: copy.start())
+    for copy in taken[5:]:
+        copy.wait()
     var_z, var_m, var_h, var_t = [
         per_panel(lambda f, c=c: variance_ref[c, 0, f]) for c in range(4)
     ]
@@ -647,11 +680,18 @@
     m_back = mc + time_increment * (east[1] + north[1]) + mass * flux_north
     t_back = tc + time_increment * (east[4] + north[4]) + geo_back
 
+    def put_copy(component, p):
+        return pltpu.make_async_copy(
+            out_ref.at[component, p], out_hbm.at[p, component, 0], put_sem.at[component, p]
+        )
+
     def put(component, tile):
         for p in range(probe_count):
             for f in range(panels):
                 start = (p * panels + f) * SUBLANES
-                out_ref[p, component, 0, f] = tile[:, start : start + SUBLANES]
+                out_ref[component, p, f] = tile[:, start : start + SUBLANES]
+        for p in range(probe_count):
+            put_copy(component, p).start()
 
     put(0, probe_z + spread_z * z_back)
     put(1, probe_m + spread_m * m_back)
@@ -670,6 +710,9 @@
         load = load + above_ref[other]
     put(2, probe_h + spread_h * (hc + u * flux_east + v * flux_north + load))
 
+    for component in range(4):
+        for p in range(probe_count):
+            put_copy(component, p).wait()
     each_send(*forward, lambda copy: copy.wait_send())
     each_send(*adjoint, lambda copy: copy.wait_send())
     for other in range(faces):
@@ -684,8 +727,9 @@
 
 def fused(count, faces, *operands):
     tile = (SUBLANES, LANES)
-    vmem = pl.BlockSpec(memory_space=pltpu.VMEM)
+    whole = pl.BlockSpec(memory_space=pl.ANY)
     probes = operands[0]
+    probe_count, components, _, panels, _, _ = probes.shape
     strips = pltpu.VMEM((4, *tile), jnp.float32)
     slots = pltpu.VMEM((8, *tile), jnp.float32)
     levels = pltpu.VMEM((faces, *tile), jnp.float32)
@@ -694,9 +738,16 @@
     return pl.pallas_call(
         functools.partial(tile_kernel, count, faces),
         out_shape=jax.ShapeDtypeStruct(probes.shape, probes.dtype),
-        in_specs=[vmem] * 6 + [pl.BlockSpec(memory_space=pltpu.SMEM)],
-        out_specs=vmem,
-        scratch_shapes=[strips] * 4
+        in_specs=[whole] * len(operands),
+        out_specs=whole,
+        scratch_shapes=[pltpu.VMEM(x.shape, x.dtype) for x in operands[:-1]]
+        + [
+            pltpu.SMEM(operands[-1].shape, operands[-1].dtype),
+            pltpu.VMEM((components, probe_count, panels, SUBLANES, SUBLANES), jnp.float32),
+            dma((len(operands),)),
+            dma((components, probe_count)),
+        ]
+        + [strips] * 4
         + [slots] * 2
         + [levels] * 2
         + [one] * 2

time: 24.5 us -> 23.4 us (0.955)
  Pallas kernels: 22.7 us -> 21.6 us
    pallas_call x1, Pallas kernels: 22.7 us -> 21.6 us  [fused(): pl.pallas_call(functools.partial(tile_kernel, count, faces), out_shape=ja...]
where the time goes in v2:
time: 23.4 us; the launch traced here: 23.2 us
  Pallas kernels  21.6 us (92%)
  local copies, waits for them, and re-layouts  1.62 us (7%)
    pallas_call x1, Pallas kernels, fused(): pl.pallas_call(functools.partial(tile_kernel, count, faces), out_shape=ja...  21.6 us
    unnamed x1, local copies, waits for them, and re-layouts  1.62 us

profile of v2, /device:TPU:0, one launch (start us, length us, event | category | flops | bytes accessed | tf_op | source)
XLA Modules:
  0.0 23.2 jit_solution(12077278067557822885)
XLA Ops:
  0.0 21.6 %shard_map.73 = f32[2,4,1,6,8,8]{5,4,3,2,1,0:T(8,128)} custom-call(f32[2,4,1,6,8,8]{5,4,3,2,1,0:T(8,128)} %probes_hbm.1, f32[2,1,6,8,8]{4,3,2,1,0:T(8,128)} %wind_hbm.1, f32[1,6,8,8]{3,2,1,0:T(8,128)} %mass_hbm.1, f32[1,6,8,8]{3,2,1,0:T(8,128)} %heat_hbm.1, f32[4,1,6,8,8]{4,3,2,1,0:T(8,128)} %spread_hbm.1, f32[4,1,6,8,8]{4,3,2,1,0:T(8,128)} %variance_hbm.1, ...), custom_call_target="tpu_custom_call" | custom-call | tf_op jit(solution)/shard_map/pallas_call | solution.py:738
  21.6 1.6 %copy.9 = f32[2,4,1,6,8,8]{5,4,3,2,1,0:T(8,128)} copy(f32[2,4,1,6,8,8]{5,4,3,2,1,0:T(8,128)} %shard_map.73) | data formatting | bytes 24576

commit v3 on v1

--- a/solution.py
+++ b/solution.py
@@ -282,6 +282,14 @@
 def tile_kernel(
     count,
     faces,
+    probes_hbm,
+    wind_hbm,
+    mass_hbm,
+    heat_hbm,
+    spread_hbm,
+    variance_hbm,
+    links_hbm,
+    out_ref,
     probes_ref,
     wind_ref,
     mass_ref,
@@ -289,23 +297,36 @@
     spread_ref,
     variance_ref,
     links_ref,
-    out_ref,
+    take_sem,
     strips_f,
     strips_a,
     halo_f,
     halo_a,
     slots_f,
     slots_a,
+    ghosts,
     below_ref,
     above_ref,
     column_f,
     column_a,
+    rows_f,
+    rows_a,
+    row_halo_f,
+    row_halo_a,
+    row_slots_f,
+    row_slots_a,
     send_f,
     send_a,
     recv_halo_f,
     recv_halo_a,
     recv_slot_f,
     recv_slot_a,
+    send_rows_f,
+    send_rows_a,
+    recv_row_halo_f,
+    recv_row_halo_a,
+    recv_row_slot_f,
+    recv_row_slot_a,
     send_below,
     send_above,
     recv_below,
@@ -343,43 +364,60 @@
 
     barrier = pltpu.get_barrier_semaphore()
 
-    def greet(place):
+    def greet(other, place):
         pl.semaphore_signal(
             barrier,
             inc=1,
-            device_id={"tx": place[0], "ty": place[1]},
+            device_id={"face": other, "tx": place[0], "ty": place[1]},
             device_id_type=MESH,
         )
 
+    for other in range(faces):
+        for d in range(4):
+            @pl.when(~at[d])
+            def _():
+                greet(other, beside[d])
+
+        @pl.when(middle)
+        def _():
+            for slot in range(8):
+                @pl.when((own_slot != slot) | (level != other))
+                def _():
+                    greet(other, slot_place(slot // 2, slot % 2))
+
+        @pl.when(corner)
+        def _():
+            for place in corners:
+                @pl.when((row != place[0]) | (column != place[1]) | (level != other))
+                def _():
+                    greet(other, place)
+
+        @pl.when(level != other)
+        def _():
+            greet(other, (row, column))
+
+    taken = [
+        pltpu.make_async_copy(source, target, take_sem.at[i])
+        for i, (source, target) in enumerate(
+            (
+                (probes_hbm, probes_ref),
+                (spread_hbm, spread_ref),
+                (wind_hbm, wind_ref),
+                (mass_hbm, mass_ref),
+                (heat_hbm, heat_ref),
+                (variance_hbm, variance_ref),
+                (links_hbm, links_ref),
+            )
+        )
+    ]
+    for copy in taken:
+        copy.start()
+
+    expected = (
+        faces - 1 + jnp.where(middle, 8 * faces - 1, 0) + jnp.where(corner, 4 * faces - 1, 0)
+    )
     for d in range(4):
-        @pl.when(~at[d])
-        def _():
-            greet(beside[d])
-
-    @pl.when(middle)
-    def _():
-        for slot in range(8):
-            @pl.when(own_slot != slot)
-            def _():
-                greet(slot_place(slot // 2, slot % 2))
-
-    @pl.when(corner)
-    def _():
-        for place in corners:
-            @pl.when((row != place[0]) | (column != place[1]))
-            def _():
-                greet(place)
-
-    for other in range(faces):
-        @pl.when(level != other)
-        def _():
-            pl.semaphore_signal(
-                barrier, inc=1, device_id={"face": other}, device_id_type=MESH
-            )
-
-    expected = faces - 1 + jnp.where(middle, 7, 0) + jnp.where(corner, 3, 0)
-    for d in range(4):
-        expected = expected + jnp.where(at[d], 0, 1)
+        expected = expected + jnp.where(at[d], 0, faces)
 
     sub = lax.broadcasted_iota(jnp.int32, (SUBLANES, LANES), 0)
     lane = lax.broadcasted_iota(jnp.int32, (SUBLANES, LANES), 1)
@@ -422,65 +460,54 @@
             other, column_a, above_ref.at[slot], send_above.at[other], recv_above.at[slot]
         )
 
-    probe_h = per_probe(2)
-    spread_h = per_panel(lambda f: spread_ref[2, 0, f])
-    h = spread_h * probe_h
-    column_f[...] = h
-    pl.semaphore_wait(barrier, expected)
-    for other in range(1, faces):
-        @pl.when(level < other)
-        def _():
-            below_copy(other, level).start()
-
-    probe_z, probe_m, probe_t = per_probe(0), per_probe(1), per_probe(3)
-    spread_z, spread_m, spread_t = [
-        per_panel(lambda f, c=c: spread_ref[c, 0, f]) for c in (0, 1, 3)
-    ]
-    u, v = [per_panel(lambda f, c=c: wind_ref[c, 0, f]) for c in range(2)]
-    mass = per_panel(lambda f: mass_ref[0, f])
-    heat = per_panel(lambda f: heat_ref[0, f])
-    z, m, t = spread_z * probe_z, spread_m * probe_m, spread_t * probe_t
-    fx = u * h + mass * z
-    fy = v * h + mass * m
+    nothing = jnp.zeros((SUBLANES, LANES), jnp.float32)
+
+    def columns_of(y_fields):
+        low = high = nothing
+        for c, field in enumerate(y_fields):
+            low = jnp.where(inner == c, rolled(field, c, 1), low)
+            high = jnp.where(inner == c, rolled(field, c - (SUBLANES - 1), 1), high)
+        return block_transposed(low, sub, inner), block_transposed(high, sub, inner)
 
     def write_strips(strips, x_fields, y_fields):
-        low = jnp.zeros((SUBLANES, LANES), jnp.float32)
-        high = low
+        low = high = nothing
         for c, field in enumerate(x_fields):
             low = jnp.where(sub == c, field[0:1, :], low)
             high = jnp.where(sub == c, field[SUBLANES - 1 : SUBLANES, :], high)
         strips[0] = low
         strips[1] = high
-        low = jnp.zeros((SUBLANES, LANES), jnp.float32)
-        high = low
-        for c, field in enumerate(y_fields):
-            low = jnp.where(inner == c, rolled(field, c, 1), low)
-            high = jnp.where(inner == c, rolled(field, c - (SUBLANES - 1), 1), high)
-        strips[2] = block_transposed(low, sub, inner)
-        strips[3] = block_transposed(high, sub, inner)
-
-    def strip_copy(source, target, send, recv, place):
+        strips[2], strips[3] = columns_of(y_fields)
+
+    def strip_copy(source, target, send, recv, other, place):
         return pltpu.make_async_remote_copy(
             src_ref=source,
             dst_ref=target,
             send_sem=send,
             recv_sem=recv,
-            device_id={"tx": place[0], "ty": place[1]},
+            device_id={"face": other, "tx": place[0], "ty": place[1]},
             device_id_type=MESH,
         )
 
-    def each_send(strips, halo, slots, send, recv_halo, recv_slot, act):
+    def each_send(buffers, act, target=None):
+        strips, halo, slots, send, recv_halo, recv_slot = buffers
+        across = target is not None
+        other = target if across else level
+        first_send = 12 * target if across else 0
+        first_halo = 4 * level if across else 0
+        first_slot = 8 * level if across else 0
+
         @pl.when(middle)
         def _():
             for slot in range(8):
-                @pl.when(own_slot != slot)
+                @pl.when((own_slot != slot) | across)
                 def _():
                     act(
                         strip_copy(
                             strips.at[own_edge],
-                            slots.at[own_slot],
-                            send.at[4 + slot],
-                            recv_slot.at[own_slot],
+                            slots.at[first_slot + own_slot],
+                            send.at[first_send + 4 + slot],
+                            recv_slot.at[first_slot + own_slot],
+                            other,
                             slot_place(slot // 2, slot % 2),
                         )
                     )
@@ -488,7 +515,7 @@
         @pl.when(corner)
         def _():
             for number, place in enumerate(corners):
-                @pl.when((row != place[0]) | (column != place[1]))
+                @pl.when((row != place[0]) | (column != place[1]) | across)
                 def _():
                     for kind, (edge, slot) in enumerate(
                         ((row_edge, row_slot), (column_edge, column_slot))
@@ -496,9 +523,10 @@
                         act(
                             strip_copy(
                                 strips.at[edge],
-                                slots.at[slot],
-                                send.at[4 + number * 2 + kind],
-                                recv_slot.at[slot],
+                                slots.at[first_slot + slot],
+                                send.at[first_send + 4 + number * 2 + kind],
+                                recv_slot.at[first_slot + slot],
+                                other,
                                 place,
                             )
                         )
@@ -509,14 +537,105 @@
                 act(
                     strip_copy(
                         strips.at[d],
-                        halo.at[d ^ 1],
-                        send.at[d],
-                        recv_halo.at[d ^ 1],
+                        halo.at[first_halo + (d ^ 1)],
+                        send.at[first_send + d],
+                        recv_halo.at[first_halo + (d ^ 1)],
+                        other,
                         beside[d],
                     )
                 )
 
-    def ghost_across(slots, edge, part, is_row, is_adjoint):
+    def each_arrival(buffers, source=None):
+        strips, halo, slots, send, recv_halo, recv_slot = buffers
+        across = source is not None
+        first_halo = 4 * source if across else 0
+        first_slot = 8 * source if across else 0
+
+        def arrival(target, semaphore):
+            strip_copy(
+                strips.at[0], target, send.at[0], semaphore, level, (row, column)
+            ).wait_recv()
+
+        for d in range(4):
+            @pl.when(~at[d])
+            def _():
+                arrival(halo.at[first_halo + d], recv_halo.at[first_halo + d])
+
+        @pl.when(on_row | on_column)
+        def _():
+            for slot in range(8):
+                mine = (on_row & (row_slot == slot)) | (on_column & (column_slot == slot))
+
+                @pl.when(~mine | across)
+                def _():
+                    arrival(slots.at[first_slot + slot], recv_slot.at[first_slot + slot])
+
+    forward = (strips_f, halo_f, slots_f, send_f, recv_halo_f, recv_slot_f)
+    adjoint = (strips_a, halo_a, slots_a, send_a, recv_halo_a, recv_slot_a)
+    forward_rows = (
+        rows_f, row_halo_f, row_slots_f, send_rows_f, recv_row_halo_f, recv_row_slot_f
+    )
+    adjoint_rows = (
+        rows_a, row_halo_a, row_slots_a, send_rows_a, recv_row_halo_a, recv_row_slot_a
+    )
+
+    def keep_own(strips, slots):
+        @pl.when(on_row)
+        def _():
+            slots[row_slot] = strips[row_edge]
+
+        @pl.when(on_column)
+        def _():
+            slots[column_slot] = strips[column_edge]
+
+    def with_levels(strip, rows, stride, index, is_adjoint):
+        if is_adjoint:
+            for other in range(1, faces):
+                strip = jnp.where(sub == 4 + other, rows[stride * other + index], strip)
+            return strip
+        beneath = jnp.zeros((1, LANES), jnp.float32)
+        for other in range(faces - 1):
+            beneath = beneath + jnp.where(level > other, rows[stride * other + index], 0.0)
+        return strip + jnp.where(sub == 4, rolled(strip, -1, 0) * beneath, 0.0)
+
+    def start(copy):
+        copy.start()
+
+    def wait_send(copy):
+        copy.wait_send()
+
+    for copy in taken[:2]:
+        copy.wait()
+    probe_h = per_probe(2)
+    spread_h = per_panel(lambda f: spread_ref[2, 0, f])
+    h = spread_h * probe_h
+    column_f[...] = h
+    rows_f[0] = h[0:1, :]
+    rows_f[1] = h[SUBLANES - 1 : SUBLANES, :]
+    low, high = columns_of((h,))
+    rows_f[2] = low[0:1, :]
+    rows_f[3] = high[0:1, :]
+    pl.semaphore_wait(barrier, expected)
+    for other in range(1, faces):
+        @pl.when(level < other)
+        def _():
+            each_send(forward_rows, start, other)
+            below_copy(other, level).start()
+
+    probe_z, probe_m, probe_t = per_probe(0), per_probe(1), per_probe(3)
+    spread_z, spread_m, spread_t = [
+        per_panel(lambda f, c=c: spread_ref[c, 0, f]) for c in (0, 1, 3)
+    ]
+    for copy in taken[2:5]:
+        copy.wait()
+    u, v = [per_panel(lambda f, c=c: wind_ref[c, 0, f]) for c in range(2)]
+    mass = per_panel(lambda f: mass_ref[0, f])
+    heat = per_panel(lambda f: heat_ref[0, f])
+    z, m, t = spread_z * probe_z, spread_m * probe_m, spread_t * probe_t
+    fx = u * h + mass * z
+    fy = v * h + mass * m
+
+    def ghost_across(slots, row_slots, edge, part, is_row, is_adjoint):
         strip = jnp.zeros((SUBLANES, LANES), jnp.float32)
         reverse = jnp.zeros((SUBLANES, LANES), jnp.int32)
         entries = [strip] * 4
@@ -524,9 +643,10 @@
             source = links_ref[f, edge, 0]
             flip = links_ref[f, edge, 2]
             slot = links_ref[f, edge, 1] * 2 + jnp.where(flip == 1, 1 - part, part)
+            held = with_levels(slots[slot], row_slots, 8, slot, is_adjoint)
             shift = (SUBLANES * (f - source) + LANES) % LANES
             here = panel_of == f
-            strip = jnp.where(here, pltpu.roll(slots[slot], shift, 1), strip)
+            strip = jnp.where(here, pltpu.roll(held, shift, 1), strip)
             reverse = jnp.where(here, flip, reverse)
             entries = [
                 jnp.where(here, links_ref[f, edge, 3 + i].astype(jnp.float32), entries[i])
@@ -545,51 +665,35 @@
         vectors = jnp.where(sub == 0, first, second)
         return jnp.where(sub < 2, vectors, jnp.where(sub == 2, normal * strip, strip))
 
-    def receive(strips, halo, slots, send, recv_halo, recv_slot, is_adjoint):
-        def arrival(target, semaphore):
-            strip_copy(strips.at[0], target, send.at[0], semaphore, (row, column)).wait_recv()
-
+    def make_ghosts(buffers, rows_buffers, is_adjoint):
+        strips, halo, slots = buffers[:3]
+        row_halo, row_slots = rows_buffers[1:3]
         for d in range(4):
             @pl.when(~at[d])
             def _():
-                arrival(halo.at[d], recv_halo.at[d])
+                ghosts[d] = with_levels(halo[d], row_halo, 4, d, is_adjoint)
 
         @pl.when(on_row)
         def _():
-            slots[row_slot] = strips[row_edge]
+            ghosts[row_edge] = ghost_across(
+                slots, row_slots, row_edge, row_part, True, is_adjoint
+            )
 
         @pl.when(on_column)
         def _():
-            slots[column_slot] = strips[column_edge]
-
-        @pl.when(on_row | on_column)
-        def _():
-            for slot in range(8):
-                mine = (on_row & (row_slot == slot)) | (on_column & (column_slot == slot))
-
-                @pl.when(~mine)
-                def _():
-                    arrival(slots.at[slot], recv_slot.at[slot])
-
-        @pl.when(on_row)
-        def _():
-            halo[row_edge] = ghost_across(slots, row_edge, row_part, True, is_adjoint)
-
-        @pl.when(on_column)
-        def _():
-            halo[column_edge] = ghost_across(
-                slots, column_edge, column_part, False, is_adjoint
-            )
-
-    def slopes_of(halo, x_fields, y_fields):
-        low, high = halo[0], halo[1]
+            ghosts[column_edge] = ghost_across(
+                slots, row_slots, column_edge, column_part, False, is_adjoint
+            )
+
+    def slopes_of(x_fields, y_fields):
+        low, high = ghosts[0], ghosts[1]
         east = []
         for c, field in enumerate(x_fields):
             before = jnp.where(sub == 0, low[c : c + 1, :], rolled(field, 1, 0))
             after = jnp.where(sub == SUBLANES - 1, high[c : c + 1, :], rolled(field, -1, 0))
             east.append(0.5 * (after - before))
-        low = block_transposed(halo[2], sub, inner)
-        high = block_transposed(halo[3], sub, inner)
+        low = block_transposed(ghosts[2], sub, inner)
+        high = block_transposed(ghosts[3], sub, inner)
         north = []
         for c, field in enumerate(y_fields):
             before = jnp.where(inner == 0, rolled(low, -c, 1), rolled(field, 1, 1))
@@ -599,30 +703,26 @@
             north.append(0.5 * (after - before))
         return east, north
 
-    forward = (strips_f, halo_f, slots_f, send_f, recv_halo_f, recv_slot_f)
-    adjoint = (strips_a, halo_a, slots_a, send_a, recv_halo_a, recv_slot_a)
-
-    for other in range(faces):
-        @pl.when(level <= other)
-        def _():
-            below_ref[other] = jnp.zeros((SUBLANES, LANES), jnp.float32)
-
-        @pl.when(level > other)
-        def _():
-            below_copy(other, other).wait_recv()
-
-    pressure = h
-    for other in range(faces):
-        pressure = pressure + below_ref[other]
-    geo = t + heat * pressure
-    x_fields, y_fields = (z, m, fx, t, geo), (z, m, fy, t, geo)
-    write_strips(strips_f, x_fields, y_fields)
-    each_send(*forward, lambda copy: copy.start())
+    geo = t + heat * h
+    write_strips(strips_f, (z, m, fx, t, geo, heat), (z, m, fy, t, geo, heat))
+    each_send(forward, start)
+    keep_own(strips_f, slots_f)
+    for copy in taken[5:]:
+        copy.wait()
     var_z, var_m, var_h, var_t = [
         per_panel(lambda f, c=c: variance_ref[c, 0, f]) for c in range(4)
     ]
-    receive(*forward, False)
-    east, north = slopes_of(halo_f, x_fields, y_fields)
+    each_arrival(forward)
+    for other in range(faces - 1):
+        @pl.when(level > other)
+        def _():
+            below_copy(other, other).wait_recv()
+            each_arrival(forward_rows, other)
+
+    for other in range(faces - 1):
+        geo = geo + heat * jnp.where(level > other, below_ref[other], 0.0)
+    make_ghosts(forward, forward_rows, False)
+    east, north = slopes_of((z, m, fx, t, geo), (z, m, fy, t, geo))
     zc = var_z * (z - time_increment * (east[4] + u * east[0] + v * north[0]))
     mc = var_m * (m - time_increment * (north[4] + u * east[1] + v * north[1]))
     hc = var_h * (h - time_increment * (east[2] + north[2]))
@@ -630,82 +730,120 @@
 
     x_fields, y_fields = (u * zc, u * mc, zc, hc, u * tc), (v * zc, v * mc, mc, hc, v * tc)
     write_strips(strips_a, x_fields, y_fields)
-    each_send(*adjoint, lambda copy: copy.start())
-    receive(*adjoint, True)
-    east, north = slopes_of(halo_a, x_fields, y_fields)
+    for d in range(4):
+        rows_a[d] = strips_a[d][2:3, :]
+    column_a[0], column_a[1], column_a[2] = zc, mc, heat
+    for other in range(faces):
+        @pl.when(level > other)
+        def _():
+            each_send(adjoint_rows, start, other)
+
+    each_send(adjoint, start)
+    for other in range(faces):
+        @pl.when(level > other)
+        def _():
+            above_copy(other, level).start()
+
+    keep_own(strips_a, slots_a)
+    each_arrival(adjoint)
+    for other in range(1, faces):
+        @pl.when(level < other)
+        def _():
+            above_copy(other, other).wait_recv()
+            each_arrival(adjoint_rows, other)
+
+    make_ghosts(adjoint, adjoint_rows, True)
+    above = [above_ref[other] for other in range(1, faces)]
+    east, north = slopes_of(
+        x_fields + tuple(tiles[0] for tiles in above),
+        y_fields + tuple(tiles[1] for tiles in above),
+    )
     geo_back = time_increment * (east[2] + north[2])
     load = heat * geo_back
-    column_a[...] = load
-    for other in range(faces):
-        @pl.when(level > other)
-        def _():
-            above_copy(other, level).start()
+    for other, tiles in enumerate(above, 1):
+        upper = tiles[2] * (time_increment * (east[4 + other] + north[4 + other]))
+        load = load + jnp.where(level < other, upper, 0.0)
 
     flux_east = time_increment * east[3]
     flux_north = time_increment * north[3]
     z_back = zc + time_increment * (east[0] + north[0]) + mass * flux_east
     m_back = mc + time_increment * (east[1] + north[1]) + mass * flux_north
     t_back = tc + time_increment * (east[4] + north[4]) + geo_back
-
-    def put(component, tile):
+    h_back = hc + u * flux_east + v * flux_north + load
+    out_ref[0] = probe_z + spread_z * z_back
+    out_ref[1] = probe_m + spread_m * m_back
+    out_ref[2] = probe_h + spread_h * h_back
+    out_ref[3] = probe_t + spread_t * t_back
+
+    each_send(forward, wait_send)
+    each_send(adjoint, wait_send)
+    for other in range(faces):
+        @pl.when(level < other)
+        def _():
+            each_send(forward_rows, wait_send, other)
+            below_copy(other, level).wait_send()
+
+        @pl.when(level > other)
+        def _():
+            each_send(adjoint_rows, wait_send, other)
+            above_copy(other, level).wait_send()
+
+
+def unpack_kernel(packed_ref, out_ref):
+    probe_count, components, _, panels, _, _ = out_ref.shape
+    for component in range(components):
+        tile = packed_ref[component]
         for p in range(probe_count):
             for f in range(panels):
                 start = (p * panels + f) * SUBLANES
                 out_ref[p, component, 0, f] = tile[:, start : start + SUBLANES]
 
-    put(0, probe_z + spread_z * z_back)
-    put(1, probe_m + spread_m * m_back)
-    put(3, probe_t + spread_t * t_back)
-
-    for other in range(faces):
-        @pl.when(level >= other)
-        def _():
-            above_ref[other] = jnp.zeros((SUBLANES, LANES), jnp.float32)
-
-        @pl.when(level < other)
-        def _():
-            above_copy(other, other).wait_recv()
-
-    for other in range(faces):
-        load = load + above_ref[other]
-    put(2, probe_h + spread_h * (hc + u * flux_east + v * flux_north + load))
-
-    each_send(*forward, lambda copy: copy.wait_send())
-    each_send(*adjoint, lambda copy: copy.wait_send())
-    for other in range(faces):
-        @pl.when(level < other)
-        def _():
-            below_copy(other, level).wait_send()
-
-        @pl.when(level > other)
-        def _():
-            above_copy(other, level).wait_send()
-
 
 def fused(count, faces, *operands):
     tile = (SUBLANES, LANES)
     vmem = pl.BlockSpec(memory_space=pltpu.VMEM)
+    whole = pl.BlockSpec(memory_space=pl.ANY)
     probes = operands[0]
     strips = pltpu.VMEM((4, *tile), jnp.float32)
     slots = pltpu.VMEM((8, *tile), jnp.float32)
-    levels = pltpu.VMEM((faces, *tile), jnp.float32)
-    one = pltpu.VMEM(tile, jnp.float32)
+
+    def edge_rows(number):
+        return pltpu.VMEM((number, 1, LANES), jnp.float32)
+
     dma = pltpu.SemaphoreType.DMA
-    return pl.pallas_call(
+    packed = pl.pallas_call(
         functools.partial(tile_kernel, count, faces),
-        out_shape=jax.ShapeDtypeStruct(probes.shape, probes.dtype),
-        in_specs=[vmem] * 6 + [pl.BlockSpec(memory_space=pltpu.SMEM)],
+        out_shape=jax.ShapeDtypeStruct((probes.shape[1], *tile), probes.dtype),
+        in_specs=[whole] * len(operands),
         out_specs=vmem,
-        scratch_shapes=[strips] * 4
+        scratch_shapes=[pltpu.VMEM(x.shape, x.dtype) for x in operands[:-1]]
+        + [
+            pltpu.SMEM(operands[-1].shape, operands[-1].dtype),
+            dma((len(operands),)),
+        ]
+        + [strips] * 4
         + [slots] * 2
-        + [levels] * 2
-        + [one] * 2
+        + [strips]
+        + [pltpu.VMEM((faces, *tile), jnp.float32), pltpu.VMEM((faces, 3, *tile), jnp.float32)]
+        + [pltpu.VMEM(tile, jnp.float32), pltpu.VMEM((3, *tile), jnp.float32)]
+        + [edge_rows(4)] * 2
+        + [edge_rows(4 * faces)] * 2
+        + [edge_rows(8 * faces)] * 2
         + [dma((12,))] * 2
         + [dma((4,))] * 2
         + [dma((8,))] * 2
+        + [dma((12 * faces,))] * 2
+        + [dma((4 * faces,))] * 2
+        + [dma((8 * faces,))] * 2
         + [dma((faces,))] * 4,
         compiler_params=pltpu.CompilerParams(collective_id=0, has_side_effects=True),
     )(*operands)
+    return pl.pallas_call(
+        unpack_kernel,
+        out_shape=jax.ShapeDtypeStruct(probes.shape, probes.dtype),
+        in_specs=[vmem],
+        out_specs=vmem,
+    )(packed)
 
 
 def solution(mesh):
@@ -718,6 +856,7 @@
             and count == mesh.shape["ty"]
             and count % 2 == 0
             and rows == columns == SUBLANES
+            and faces + 4 <= SUBLANES
             and probe_count * panels * SUBLANES < LANES
         )
         return fused(count, faces, *operands) if fits else body(*operands)

time: 24.5 us -> 20.7 us (0.84)
  Pallas kernels: 22.7 us -> 20.5 us
  local copies, waits for them, and re-layouts: 1.62 us -> 0 us
    pallas_call x1, Pallas kernels: 22.7 us -> 19 us  [fused(): pl.pallas_call(functools.partial(tile_kernel, count, faces), out_shape=ja...]
    unnamed x1 -> x0, local copies, waits for them, and re-layouts: 1.62 us -> none
    pallas_call x0 -> x1, Pallas kernels: none -> 1.51 us  [fused(): pl.pallas_call(unpack_kernel, out_shape=jax.ShapeDtypeStruct(probes.shape...]
where the time goes in v3:
time: 20.7 us; the launch traced here: 20.5 us
  Pallas kernels  20.5 us (99%)
    pallas_call x1, Pallas kernels, fused(): pl.pallas_call(functools.partial(tile_kernel, count, faces), out_shape=ja...  19 us
    pallas_call x1, Pallas kernels, fused(): pl.pallas_call(unpack_kernel, out_shape=jax.ShapeDtypeStruct(probes.shape...  1.51 us

profile of v3, /device:TPU:0, one launch (start us, length us, event | category | flops | bytes accessed | tf_op | source)
XLA Modules:
  0.0 20.5 jit_solution(18213944724911220451)
XLA Ops:
  0.0 19.0 %shard_map.73.packed_ref = f32[4,8,128]{2,1,0:T(8,128)} custom-call(f32[2,4,1,6,8,8]{5,4,3,2,1,0:T(8,128)} %probes_hbm.1, f32[2,1,6,8,8]{4,3,2,1,0:T(8,128)} %wind_hbm.1, f32[1,6,8,8]{3,2,1,0:T(8,128)} %mass_hbm.1, f32[1,6,8,8]{3,2,1,0:T(8,128)} %heat_hbm.1, f32[4,1,6,8,8]{4,3,2,1,0:T(8,128)} %spread_hbm.1, f32[4,1,6,8,8]{4,3,2,1,0:T(8,128)} %variance_hbm.1, ...), custom_call_target="tpu_custom_call" | custom-call | tf_op jit(solution)/shard_map/pallas_call | solution.py:814
  19.0 1.5 %shard_map.74 = f32[2,4,1,6,8,8]{5,4,3,2,1,0:T(8,128)} custom-call(f32[4,8,128]{2,1,0:T(8,128)} %shard_map.73.packed_ref), custom_call_target="tpu_custom_call" | custom-call | tf_op jit(solution)/shard_map/pallas_call | solution.py:841

commit v4 on v3

--- a/solution.py
+++ b/solution.py
@@ -10,6 +10,7 @@
 MESH = pl.DeviceIdType.MESH
 SUBLANES = 8
 LANES = 128
+VMEM_BYTES = 4 * 2**20
 
 time_increment = 0.3
 forward_layout = (("vector", 0), ("vector", 2), ("scalar", 4), ("scalar", 5))
@@ -813,7 +814,7 @@
     dma = pltpu.SemaphoreType.DMA
     packed = pl.pallas_call(
         functools.partial(tile_kernel, count, faces),
-        out_shape=jax.ShapeDtypeStruct((probes.shape[1], *tile), probes.dtype),
+        out_shape=pltpu.VMEM((probes.shape[1], *tile), probes.dtype),
         in_specs=[whole] * len(operands),
         out_specs=vmem,
         scratch_shapes=[pltpu.VMEM(x.shape, x.dtype) for x in operands[:-1]]
@@ -843,6 +844,7 @@
         out_shape=jax.ShapeDtypeStruct(probes.shape, probes.dtype),
         in_specs=[vmem],
         out_specs=vmem,
+        compiler_params=pltpu.CompilerParams(vmem_limit_bytes=VMEM_BYTES),
     )(packed)
 
 

time: 20.7 us -> 19.3 us (0.932)
  Pallas kernels: 20.5 us -> 19.2 us
    pallas_call x1, Pallas kernels: 1.51 us -> 0.79 us  [fused(): pl.pallas_call(unpack_kernel, out_shape=jax.ShapeDtypeStruct(probes.shape...]
    pallas_call x1, Pallas kernels: 19 us -> 18.4 us  [fused(): pl.pallas_call(functools.partial(tile_kernel, count, faces), out_shape=pl...]
where the time goes in v4:
time: 19.3 us; the launch traced here: 19.2 us
  Pallas kernels  19.2 us (99%)
    pallas_call x1, Pallas kernels, fused(): pl.pallas_call(functools.partial(tile_kernel, count, faces), out_shape=pl...  18.4 us
    pallas_call x1, Pallas kernels, fused(): pl.pallas_call(unpack_kernel, out_shape=jax.ShapeDtypeStruct(probes.shape...  0.79 us

profile of v4, /device:TPU:0, one launch (start us, length us, event | category | flops | bytes accessed | tf_op | source)
XLA Modules:
  0.0 19.2 jit_solution(1869725508828770808)
XLA Ops:
  0.0 18.4 %shard_map.73.packed_ref = f32[4,8,128]{2,1,0:T(8,128)S(1)} custom-call(f32[2,4,1,6,8,8]{5,4,3,2,1,0:T(8,128)} %probes_hbm.1, f32[2,1,6,8,8]{4,3,2,1,0:T(8,128)} %wind_hbm.1, f32[1,6,8,8]{3,2,1,0:T(8,128)} %mass_hbm.1, f32[1,6,8,8]{3,2,1,0:T(8,128)} %heat_hbm.1, f32[4,1,6,8,8]{4,3,2,1,0:T(8,128)} %spread_hbm.1, f32[4,1,6,8,8]{4,3,2,1,0:T(8,128)} %variance_hbm.1, ...), custom_call_target="tpu_custom_call" | custom-call | tf_op jit(solution)/shard_map/pallas_call | solution.py:815
  18.4 0.8 %shard_map.74 = f32[2,4,1,6,8,8]{5,4,3,2,1,0:T(8,128)} custom-call(f32[4,8,128]{2,1,0:T(8,128)S(1)} %shard_map.73.packed_ref), custom_call_target="tpu_custom_call" | custom-call | tf_op jit(solution)/shard_map/pallas_call | solution.py:842

commit v5 on v4

--- a/solution.py
+++ b/solution.py
@@ -258,26 +258,21 @@
     return pltpu.roll(tile, shift % tile.shape[axis], axis)
 
 
+def gathered(tile, index, axis):
+    return jnp.take_along_axis(tile, index, axis=axis, mode="promise_in_bounds")
+
+
 def block_transposed(tile, sub, inner):
-    step = SUBLANES // 2
-    while step:
-        ahead = rolled(rolled(tile, -step, 0), step, 1)
-        behind = rolled(rolled(tile, step, 0), -step, 1)
-        low_row = (sub & step) == 0
-        low_lane = (inner & step) == 0
-        tile = jnp.where(low_row == low_lane, tile, jnp.where(low_row, ahead, behind))
-        step //= 2
-    return tile
+    base = lax.broadcasted_iota(jnp.int32, tile.shape, 1) - inner
+    skew = (inner - sub + SUBLANES) % SUBLANES
+    tile = gathered(tile, base + skew, 1)
+    tile = gathered(tile, skew, 0)
+    return gathered(tile, base + (inner + sub) % SUBLANES, 1)
 
 
 def block_reversed(tile, inner):
-    step = SUBLANES // 2
-    while step:
-        tile = jnp.where(
-            (inner & step) == 0, rolled(tile, -step, 1), rolled(tile, step, 1)
-        )
-        step //= 2
-    return tile
+    lane = lax.broadcasted_iota(jnp.int32, tile.shape, 1)
+    return gathered(tile, lane - inner + (SUBLANES - 1 - inner), 1)
 
 
 def tile_kernel(

time: 19.3 us -> 18.5 us (0.959)
  Pallas kernels: 19.2 us -> 18.3 us
    pallas_call x1, Pallas kernels: 18.4 us -> 17.5 us  [fused(): pl.pallas_call(functools.partial(tile_kernel, count, faces), out_shape=pl...]
where the time goes in v5:
time: 18.5 us; the launch traced here: 18.3 us
  Pallas kernels  18.3 us (99%)
    pallas_call x1, Pallas kernels, fused(): pl.pallas_call(functools.partial(tile_kernel, count, faces), out_shape=pl...  17.5 us
    pallas_call x1, Pallas kernels, fused(): pl.pallas_call(unpack_kernel, out_shape=jax.ShapeDtypeStruct(probes.shape...  0.79 us

profile of v5, /device:TPU:0, one launch (start us, length us, event | category | flops | bytes accessed | tf_op | source)
XLA Modules:
  0.0 18.3 jit_solution(14327157830868537093)
XLA Ops:
  0.0 17.5 %shard_map.73.packed_ref = f32[4,8,128]{2,1,0:T(8,128)S(1)} custom-call(f32[2,4,1,6,8,8]{5,4,3,2,1,0:T(8,128)} %probes_hbm.1, f32[2,1,6,8,8]{4,3,2,1,0:T(8,128)} %wind_hbm.1, f32[1,6,8,8]{3,2,1,0:T(8,128)} %mass_hbm.1, f32[1,6,8,8]{3,2,1,0:T(8,128)} %heat_hbm.1, f32[4,1,6,8,8]{4,3,2,1,0:T(8,128)} %spread_hbm.1, f32[4,1,6,8,8]{4,3,2,1,0:T(8,128)} %variance_hbm.1, ...), custom_call_target="tpu_custom_call" | custom-call | tf_op jit(solution)/shard_map/pallas_call | solution.py:810
  17.5 0.8 %shard_map.74 = f32[2,4,1,6,8,8]{5,4,3,2,1,0:T(8,128)} custom-call(f32[4,8,128]{2,1,0:T(8,128)S(1)} %shard_map.73.packed_ref), custom_call_target="tpu_custom_call" | custom-call | tf_op jit(solution)/shard_map/pallas_call | solution.py:837
